TPU v7x, 32 devices: a whole 2x2x4 slice. The times are simulated.
32 devices in a mesh: dp: 8 (over z, y), tensor: 4 (over x, core).
Axes of the slice: x: 2, y: 2, z: 4, core: 2. Of those that a mesh axis runs over, the one named last changes fastest.
Arguments:
- hidden_states: bfloat16 [16, 320, 1024], P('dp', None, 'tensor'), may hold values from -6 to 6
- output_grad: bfloat16 [16, 320, 1024], P('dp', None, 'tensor'), may hold values from -6 to 6
- group_counts: int32 [8], P('dp'), may hold values from 1 to 2, as said below
- gain_attention: float32 [1024], replicated, may hold values from 0.5 to 1.5
- shift_attention: float32 [1024], replicated, may hold values from -3 to 3
- gain_feedforward: float32 [1024], replicated, may hold values from 0.5 to 1.5
- shift_feedforward: float32 [1024], replicated, may hold values from -3 to 3
- heads_weight: bfloat16 [1024, 3, 1024], P(None, None, 'tensor'), may hold values from -0.1875 to 0.1875
- heads_bias: float32 [3, 1024], P(None, 'tensor'), may hold values from -3 to 3
- merge_weight: bfloat16 [1024, 1024], P('tensor'), may hold values from -0.75 to 0.75
- merge_bias: float32 [1024], P('tensor'), may hold values from -3 to 3
- expand_weight: bfloat16 [1024, 4096], P(None, 'tensor'), may hold values from -0.1875 to 0.1875
- expand_bias: float32 [4096], P('tensor'), may hold values from -3 to 3
- contract_weight: bfloat16 [4096, 1024], P('tensor'), may hold values from -0.09375 to 0.09375
- contract_bias: float32 [1024], P('tensor'), may hold values from -3 to 3
Outputs:
- block_output: bfloat16 [16, 320, 1024], P('dp', None, 'tensor')
- input_grad: bfloat16 [16, 320, 1024], P('dp', None, 'tensor')
- grad_gain_attention: float32 [1024], P('tensor')
- grad_shift_attention: float32 [1024], P('tensor')
- grad_gain_feedforward: float32 [1024], P('tensor')
- grad_shift_feedforward: float32 [1024], P('tensor')
- grad_heads_weight: float32 [1024, 3, 1024], P('dp', None, 'tensor')
- grad_heads_bias: float32 [3, 1024], P(None, 'tensor')
- grad_merge_weight: float32 [1024, 1024], P('tensor', 'dp')
- grad_merge_bias: float32 [1024], P('tensor')
- grad_expand_weight: float32 [1024, 4096], P('dp', 'tensor')
- grad_expand_bias: float32 [4096], P('tensor')
- grad_contract_weight: float32 [4096, 1024], P('tensor', 'dp')
- grad_contract_bias: float32 [1024], P('tensor')
Inputs may be any that keep to these rules, and one draw needn't show every extreme that they name: `group_counts`: each index of dp has 1 or 2 live sequences in its first slots; slots after them are padding, and at least one index has 2.
All inputs are finite; a program needn't handle non-finite values.
Results may differ from a plain program's by a relative error of at most 0.015.
Values may be sent and summed in bfloat16 or wider, within the bound.
A program may use at most 128 MiB of HBM per device.

v0:
```python
import math

import jax
import jax.numpy as jnp
from jax import lax
from jax.sharding import PartitionSpec as P

HEAD_DIM = 64
ROT = 16


EPSILON = 1e-05


def rotary_tables(length):
    half_rot = ROT // 2
    position = jnp.arange(length, dtype=jnp.float32)[:, None]
    exponent = jnp.arange(half_rot, dtype=jnp.float32) * (2.0 / ROT)
    angles = position * jnp.exp(-math.log(10000.0) * exponent)[None, :]
    return (jnp.cos(angles), jnp.sin(angles))


def rotate_heads(values, cosine_table, sine_table, direction):
    half_rot = ROT // 2
    leading = values[..., :half_rot]
    trailing = values[..., half_rot:ROT]
    remainder = values[..., ROT:]
    turned = sine_table * direction
    return jnp.concatenate(
        [
            leading * cosine_table - trailing * turned,
            trailing * cosine_table + leading * turned,
            remainder,
        ],
        axis=-1,
    )


def gelu_value(hidden):
    return 0.5 * hidden * (1.0 + lax.erf(hidden * 0.7071067811865476))


def gelu_slope(hidden):
    return (
        0.5 * (1.0 + lax.erf(hidden * 0.7071067811865476))
        + hidden * jnp.exp(-0.5 * hidden * hidden) * 0.3989422804014327
    )


def norm_forward(values, gain, offset):
    center = jnp.mean(values, axis=-1, keepdims=True)
    shifted = values - center
    inverse = lax.rsqrt(jnp.mean(shifted * shifted, axis=-1, keepdims=True) + EPSILON)
    normed = shifted * inverse
    return (normed, inverse, normed * gain + offset)


def causal_scores(query, keys):
    scores = jnp.einsum("bhqd,bhkd->bhqk", query, keys, preferred_element_type=jnp.float32)
    length = scores.shape[-1]
    allowed = jnp.arange(length)[:, None] >= jnp.arange(length)[None, :]
    return jnp.where(allowed, scores, -1e30)


def own_columns(array, start, count):
    return lax.dynamic_slice_in_dim(array, start, count, axis=array.ndim - 1)


def body(
    hidden_states,
    output_grad,
    group_counts,
    gain_attention,
    shift_attention,
    gain_feedforward,
    shift_feedforward,
    heads_weight,
    heads_bias,
    merge_weight,
    merge_bias,
    expand_weight,
    expand_bias,
    contract_weight,
    contract_bias,
):
    slots, length, local_width = hidden_states.shape
    width = gain_attention.shape[0]
    rows = slots * length
    local_heads = local_width // HEAD_DIM
    head_scale = 1.0 / math.sqrt(HEAD_DIM)
    start = lax.axis_index("tensor") * local_width
    full_states, full_grad = (
        lax.all_gather(hidden_states, "tensor", axis=2, tiled=True),
        lax.all_gather(output_grad, "tensor", axis=2, tiled=True),
    )
    live = (jnp.arange(slots) < group_counts[0]).astype(jnp.float32)
    cosine_table, sine_table = rotary_tables(length)
    residual = full_states.astype(jnp.float32).reshape(rows, width)
    normed_one, inverse_one, attn_norm = norm_forward(residual, gain_attention, shift_attention)
    normed_two, inverse_two, ffn_norm = norm_forward(residual, gain_feedforward, shift_feedforward)
    attn_input = attn_norm.astype(jnp.bfloat16)
    ffn_input = ffn_norm.astype(jnp.bfloat16)
    flat_heads = heads_weight.reshape(width, 3 * local_width)
    projected = jnp.dot(attn_input, flat_heads, preferred_element_type=jnp.float32).reshape(
        slots, length, 3, local_heads, HEAD_DIM
    ) + heads_bias.reshape(3, local_heads, HEAD_DIM)
    query = (
        rotate_heads(jnp.transpose(projected[:, :, 0], (0, 2, 1, 3)), cosine_table, sine_table, 1.0)
        * head_scale
    ).astype(jnp.bfloat16)
    keys = rotate_heads(
        jnp.transpose(projected[:, :, 1], (0, 2, 1, 3)), cosine_table, sine_table, 1.0
    ).astype(jnp.bfloat16)
    values = jnp.transpose(projected[:, :, 2], (0, 2, 1, 3)).astype(jnp.bfloat16)
    scores = causal_scores(query, keys)
    row_peak = jnp.max(scores, axis=-1, keepdims=True)
    logsum = row_peak + jnp.log(jnp.sum(jnp.exp(scores - row_peak), axis=-1, keepdims=True))
    probs = jnp.exp(scores - logsum).astype(jnp.bfloat16)
    context = jnp.einsum(
        "bhqk,bhkd->bhqd", probs, values, preferred_element_type=jnp.float32
    ).astype(jnp.bfloat16)
    context_rows = jnp.transpose(context, (0, 2, 1, 3)).reshape(rows, local_width)
    attn_part = jnp.dot(context_rows, merge_weight, preferred_element_type=jnp.float32)
    pre_active = jnp.dot(ffn_input, expand_weight, preferred_element_type=jnp.float32) + expand_bias
    active = gelu_value(pre_active).astype(jnp.bfloat16)
    ffn_part = jnp.dot(active, contract_weight, preferred_element_type=jnp.float32)
    summed = lax.psum_scatter(
        (attn_part + ffn_part).reshape(slots, length, width),
        "tensor",
        scatter_dimension=2,
        tiled=True,
    )
    block_output = (hidden_states.astype(jnp.float32) + summed + merge_bias + contract_bias).astype(
        jnp.bfloat16
    )
    masked = (
        (full_grad.astype(jnp.float32) * live[:, None, None])
        .astype(jnp.bfloat16)
        .reshape(rows, width)
    )
    own_masked = (output_grad.astype(jnp.float32) * live[:, None, None]).reshape(rows, local_width)
    grad_out_bias = jnp.sum(own_masked, axis=0)
    grad_merge = jnp.dot(context_rows.T, masked, preferred_element_type=jnp.float32)
    grad_contract = jnp.dot(active.T, masked, preferred_element_type=jnp.float32)
    active_grad = jnp.dot(
        masked, contract_weight.T, preferred_element_type=jnp.float32
    ) * gelu_slope(pre_active)
    grad_expand_bias = jnp.sum(active_grad, axis=0)
    active_grad16 = active_grad.astype(jnp.bfloat16)
    grad_expand = jnp.dot(ffn_input.T, active_grad16, preferred_element_type=jnp.float32)
    ffn_back = jnp.dot(active_grad16, expand_weight.T, preferred_element_type=jnp.float32)
    context_grad = jnp.dot(masked, merge_weight.T, preferred_element_type=jnp.float32).astype(
        jnp.bfloat16
    )
    context_grad = jnp.transpose(
        context_grad.reshape(slots, length, local_heads, HEAD_DIM), (0, 2, 1, 3)
    )
    probs_again = jnp.exp(causal_scores(query, keys) - logsum)
    prob_grad = jnp.einsum(
        "bhqd,bhkd->bhqk", context_grad, values, preferred_element_type=jnp.float32
    )
    delta = jnp.sum(
        context_grad.astype(jnp.float32) * context.astype(jnp.float32), axis=-1, keepdims=True
    )
    score_grad = (probs_again * (prob_grad - delta)).astype(jnp.bfloat16)
    query_grad = (
        jnp.einsum("bhqk,bhkd->bhqd", score_grad, keys, preferred_element_type=jnp.float32)
        * head_scale
    )
    keys_grad = jnp.einsum("bhqk,bhqd->bhkd", score_grad, query, preferred_element_type=jnp.float32)
    values_grad = jnp.einsum(
        "bhqk,bhqd->bhkd", probs, context_grad, preferred_element_type=jnp.float32
    )
    query_grad = rotate_heads(query_grad, cosine_table, sine_table, -1.0)
    keys_grad = rotate_heads(keys_grad, cosine_table, sine_table, -1.0)
    heads_grad = jnp.transpose(
        jnp.stack([query_grad, keys_grad, values_grad], axis=1), (0, 3, 1, 2, 4)
    ).reshape(rows, 3 * local_width)
    grad_heads_bias = jnp.sum(heads_grad, axis=0).reshape(3, local_width)
    heads_grad16 = heads_grad.astype(jnp.bfloat16)
    grad_heads = jnp.dot(attn_input.T, heads_grad16, preferred_element_type=jnp.float32).reshape(
        width, 3, local_width
    )
    attn_back = jnp.dot(heads_grad16, flat_heads.T, preferred_element_type=jnp.float32)
    sent_heads, sent_merge, sent_expand, sent_contract = (
        lax.psum_scatter(grad_heads, "dp", scatter_dimension=0, tiled=True),
        lax.psum_scatter(grad_merge, "dp", scatter_dimension=1, tiled=True),
        lax.psum_scatter(grad_expand, "dp", scatter_dimension=0, tiled=True),
        lax.psum_scatter(grad_contract, "dp", scatter_dimension=1, tiled=True),
    )
    share_one, share_two = (
        lax.psum_scatter(attn_back, "tensor", scatter_dimension=1, tiled=True),
        lax.psum_scatter(ffn_back, "tensor", scatter_dimension=1, tiled=True),
    )
    normed_one_own = own_columns(normed_one, start, local_width)
    normed_two_own = own_columns(normed_two, start, local_width)
    scaled_one = share_one * own_columns(gain_attention, start, local_width)
    scaled_two = share_two * own_columns(gain_feedforward, start, local_width)
    stats = lax.psum(
        (
            jnp.sum(scaled_one, axis=-1),
            jnp.sum(scaled_one * normed_one_own, axis=-1),
            jnp.sum(scaled_two, axis=-1),
            jnp.sum(scaled_two * normed_two_own, axis=-1),
        ),
        "tensor",
    )
    input_one = inverse_one * (
        scaled_one - stats[0][:, None] / width - normed_one_own * (stats[1][:, None] / width)
    )
    input_two = inverse_two * (
        scaled_two - stats[2][:, None] / width - normed_two_own * (stats[3][:, None] / width)
    )
    input_grad = own_masked + input_one + input_two
    gain_one = jnp.sum(share_one * normed_one_own, axis=0)
    shift_one = jnp.sum(share_one, axis=0)
    gain_two = jnp.sum(share_two * normed_two_own, axis=0)
    shift_two = jnp.sum(share_two, axis=0)
    vectors = lax.psum(
        (
            gain_one,
            shift_one,
            gain_two,
            shift_two,
            grad_out_bias,
            grad_heads_bias,
            grad_expand_bias,
        ),
        "dp",
    )
    input_grad = input_grad.astype(jnp.bfloat16).reshape(slots, length, local_width)
    return (
        block_output,
        input_grad,
        vectors[0],
        vectors[1],
        vectors[2],
        vectors[3],
        sent_heads,
        vectors[5],
        sent_merge,
        vectors[4],
        sent_expand,
        vectors[6],
        sent_contract,
        vectors[4],
    )


def solution(mesh):
    placed = (
        P("dp", None, "tensor"),
        P("dp", None, "tensor"),
        P("dp"),
        P(),
        P(),
        P(),
        P(),
        P(None, None, "tensor"),
        P(None, "tensor"),
        P("tensor", None),
        P("tensor"),
        P(None, "tensor"),
        P("tensor"),
        P("tensor", None),
        P("tensor"),
    )
    return jax.shard_map(
        body,
        mesh=mesh,
        in_specs=placed,
        out_specs=(
            P("dp", None, "tensor"),
            P("dp", None, "tensor"),
            P("tensor"),
            P("tensor"),
            P("tensor"),
            P("tensor"),
            P("dp", None, "tensor"),
            P(None, "tensor"),
            P("tensor", "dp"),
            P("tensor"),
            P("dp", "tensor"),
            P("tensor"),
            P("tensor", "dp"),
            P("tensor"),
        ),
        check_vma=False,
    )
```

profile of v0, /device:TPU:0, one launch (start us, length us, event | category | flops | bytes accessed | tf_op | source)
XLA Modules:
  0.0 527.7 jit_solution(17933904790477624768)
XLA Ops:
  10.7 2.6 copy.36
  13.9 16.7 %all-gather.3.cloned.1.call-done = bf16[2,320,1024]{2,1,0:T(8,128)(2,1)} async-done(((bf16[2,320,256]{2,1,0:T(8,128)(2,1)}), bf16[2,320,1024]{2,1,0:T(8,128)(2,1)}) %all-gather.3.cloned.1.call-update) | async-done | bytes 1310736 | tf_op jit(solution)/shard_map/all_gather | solution.py:93
  30.6 1.7 convert_reduce_fusion
  32.4 1.8 multiply_reduce_fusion
  34.2 1.2 add_convert_fusion.1
  35.5 1.4 convolution_add_fusion.1
  36.9 1.4 copy-done.8
  38.5 0.9 copy-done.12
  39.4 0.9 slice.66
  41.1 9.5 %all-gather.5.cloned.1.call-done = bf16[2,320,1024]{2,1,0:T(8,128)(2,1)} async-done(((bf16[2,320,256]{2,1,0:T(8,128)(2,1)}), bf16[2,320,1024]{2,1,0:T(8,128)(2,1)}) %all-gather.5.cloned.1.call-update) | async-done | bytes 1310736 | tf_op jit(solution)/shard_map/all_gather | solution.py:94
  50.5 1.9 multiply_convert_fusion.1
  52.4 1.1 copy-done.6
  53.6 1.3 convolution_convert_fusion.1
  54.8 2.3 reshape.246
  57.1 2.0 copy.41
  59.1 1.1 multiply_subtract_fusion.2
  60.2 2.0 select_reduce_fusion
  63.0 0.9 copy-done.9
  63.9 1.9 multiply_reduce_fusion.1
  65.8 1.3 multiply_convert_fusion
  68.5 1.0 convolution_bitcast_fusion
  71.3 2.2 copy.46
  73.6 3.6 convert_element_type.105
  77.1 4.4 fusion.38
  82.3 2.9 multiply_convert_fusion.2
  85.7 2.6 fusion.36
  88.3 1.1 copy-done.36
  89.4 3.1 fusion.15
  92.6 2.1 copy.39
  94.7 2.0 reshape.235
  96.7 3.6 fusion.37
  100.4 2.0 convolution_add_fusion
  102.5 2.5 fusion.40
  105.1 4.8 fusion.39
  110.0 5.9 %fusion.13 = f32[1024,1024]{1,0:T(8,128)} fusion(bf16[640,1024]{1,0:T(8,128)(2,1)} %copy-done.36, f32[640,1024]{1,0:T(8,128)} %copy-done.5, f32[1024]{0:T(1024)S(1)} %copy-done.35, f32[1024]{0:T(1024)S(1)} %copy-done.32), kind=kOutput, calls=%fused_computation.44 | convolution fusion | flops 1344143360 | bytes 8134656 | tf_op jit(solution)/shard_map/dot_general | solution.py:150
  116.2 5.1 fusion.41
  122.3 1.0 fusion.32
  123.3 1.7 fusion.7
  125.1 27.8 %reduce-scatter.12.cloned.1.call-done = f32[640,256]{1,0:T(8,128)} async-done(((f32[640,1024]{1,0:T(8,128)}), f32[640,256]{1,0:T(8,128)}) %reduce-scatter.12.cloned.1.call-update) | async-done | bytes 655376 | tf_op jit(solution)/shard_map/reduce_scatter | solution.py:193
  152.9 2.0 multiply_reduce_fusion.2
  155.0 37.6 %all-reduce = (f32[256]{0:T(256)}, f32[256]{0:T(256)}, f32[256]{0:T(256)}, f32[256]{0:T(256)}, f32[3,256]{1,0:T(4,128)}, /*index=5*/f32[256]{0:T(256)S(1)}, f32[1024]{0:T(1024)}) all-reduce(f32[256]{0:T(256)S(1)} %get-tuple-element.19, f32[256]{0:T(256)S(1)} %get-tuple-element.22, ...), channel_id=1, replica_groups=mesh['dp'=8,'tensor'=4] {'dp'}, use_global_device_ids=true, to_apply=%region_17.18 | all-reduce | flops 3072 | bytes 24576 | tf_op jit(solution)/shard_map/psum | solution.py:219
  192.6 10.2 %all-reduce.1 = (f32[640]{0:T(1024)S(1)}, f32[640]{0:T(1024)S(1)}, f32[640]{0:T(1024)S(1)}, f32[640]{0:T(1024)S(1)}) all-reduce(f32[640]{0:T(1024)S(1)} %get-tuple-element.15, f32[640]{0:T(1024)S(1)} %get-tuple-element.21, f32[640]{0:T(1024)S(1)} %get-tuple-element.18, ...), channel_id=1, replica_groups=mesh['dp'=8,'tensor'=4] {'tensor'}, use_global_device_ids=true, to_apply=%region_15.16 | all-reduce | flops 2560 | bytes 20480 | tf_op jit(solution)/shard_map/psum | solution.py:199
  202.9 2.0 add_convert_fusion.2
  204.9 2.5 fusion.12
  207.4 50.9 %reduce-scatter.16.cloned.1.call-done = f32[256,128]{1,0:T(8,128)} async-done(((f32[256,1024]{1,0:T(8,128)}), f32[256,128]{1,0:T(8,128)}) %reduce-scatter.16.cloned.1.call-update) | async-done | bytes 131088 | tf_op jit(solution)/shard_map/reduce_scatter | solution.py:187
  258.3 78.2 %reduce-scatter.14.cloned.1.call-done = f32[128,3,256]{2,0,1:T(8,128)} async-done(((f32[1024,3,256]{2,0,1:T(8,128)}), f32[128,3,256]{2,0,1:T(8,128)}) %reduce-scatter.14.cloned.1.call-update) | async-done | bytes 393232 | tf_op jit(solution)/shard_map/reduce_scatter | solution.py:186
  336.4 91.6 %reduce-scatter.18.cloned.1.call-done = f32[128,1024]{1,0:T(8,128)} async-done(((f32[1024,1024]{1,0:T(8,128)}), f32[128,1024]{1,0:T(8,128)}) %reduce-scatter.18.cloned.1.call-update) | async-done | bytes 524304 | tf_op jit(solution)/shard_map/reduce_scatter | solution.py:188
  428.1 92.5 %reduce-scatter.20.cloned.1.call-done = f32[1024,128]{1,0:T(8,128)} async-done(((f32[1024,1024]{1,0:T(8,128)}), f32[1024,128]{1,0:T(8,128)}) %reduce-scatter.20.cloned.1.call-update) | async-done | bytes 524304 | tf_op jit(solution)/shard_map/reduce_scatter | solution.py:189
  (118 shorter events, 11.8 us)
Async XLA Ops:
  7.2 75.0 %copy-start = (bf16[1024,1024]{1,0:T(8,128)(2,1)S(1)}, bf16[1024,1024]{1,0:T(8,128)(2,1)}, u32[]{:S(2)}) copy-start(bf16[1024,1024]{1,0:T(8,128)(2,1)} %param.26) | copy-start | bytes 6291460
  7.2 6.0 %copy-start.27 = (f32[3,256]{1,0:T(4,128)S(1)}, f32[3,256]{1,0:T(4,128)}, u32[]{:S(2)}) copy-start(f32[3,256]{1,0:T(4,128)} %param.23) | copy-start | bytes 9220
  7.2 23.4 %all-gather.3.cloned.1.call-start = ((), (), s32[]{:S(2)}) async-start(), calls=%async_computation.7 | async-start | bytes 1638400 | tf_op jit(solution)/shard_map/all_gather | solution.py:93
  7.9 42.6 %all-gather.5.cloned.1.call-start = ((), (), s32[]{:S(2)}) async-start(), calls=%async_computation.9 | async-start | bytes 1638400 | tf_op jit(solution)/shard_map/all_gather | solution.py:94
  8.7 116.4 %reduce-scatter.10.cloned.1.call-start = ((), (), s32[]{:S(2)}) async-start(), calls=%async_computation.10 | async-start | bytes 3276800 | tf_op jit(solution)/shard_map/reduce_scatter | solution.py:192
  10.6 23.5 %copy-start.25 = (f32[1024]{0:T(1024)S(1)}, f32[1024]{0:T(1024)}, u32[]{:S(2)}) copy-start(f32[1024]{0:T(1024)} %param.18) | copy-start | bytes 12292
  30.6 3.6 copy-start.1
  30.6 4.8 copy-start.18
  30.6 4.8 copy-start.26
  35.4 1.5 copy-start.19
  36.9 1.4 copy-start.8
  38.5 0.9 copy-start.12
  38.5 1.9 copy-start.17
  50.5 3.0 copy-start.22
  52.4 1.1 copy-start.6
  62.2 1.7 copy-start.9
  62.2 1.7 copy-start.10
  65.8 1.3 copy-start.16
  67.1 1.0 copy-start.21
  68.5 1.1 copy-start.24
  69.5 0.9 copy-start.11
  69.9 0.9 copy-start.2
  69.9 1.2 copy-start.4
  81.5 0.7 copy-start.32
  81.6 0.7 copy-start.34
  81.6 0.7 copy-start.35
  81.6 71.3 %reduce-scatter.12.cloned.1.call-start = ((), (), s32[]{:S(2)}) async-start(), calls=%async_computation.11 | async-start | bytes 3276800 | tf_op jit(solution)/shard_map/reduce_scatter | solution.py:193
  82.3 2.9 copy-start.5
  82.3 2.9 copy-start.7
  82.3 3.4 copy-start.33
  88.3 1.1 copy-start.36
  92.5 110.3 %reduce-scatter.8.cloned.1.call-start = ((), (), s32[]{:S(2)}) async-start(), calls=%async_computation.8 | async-start | bytes 3276800 | tf_op jit(solution)/shard_map/reduce_scatter | solution.py:127
  96.7 3.6 copy-start.13
  96.7 3.6 copy-start.23
  102.4 155.8 %reduce-scatter.16.cloned.1.call-start = ((), (), s32[]{:S(2)}) async-start(), calls=%async_computation.13 | async-start | bytes 1179648 | tf_op jit(solution)/shard_map/reduce_scatter | solution.py:187
  105.0 231.4 %reduce-scatter.14.cloned.1.call-start = ((), (), s32[]{:S(2)}) async-start(), calls=%async_computation.12 | async-start | bytes 3538944 | tf_op jit(solution)/shard_map/reduce_scatter | solution.py:186
  109.9 318.1 %reduce-scatter.18.cloned.1.call-start = ((), (), s32[]{:S(2)}) async-start(), calls=%async_computation.14 | async-start | bytes 4718592 | tf_op jit(solution)/shard_map/reduce_scatter | solution.py:188
  115.9 404.7 %reduce-scatter.20.cloned.1.call-start = ((), (), s32[]{:S(2)}) async-start(), calls=%async_computation.15 | async-start | bytes 4718592 | tf_op jit(solution)/shard_map/reduce_scatter | solution.py:189
  121.3 1.0 copy-start.20
  121.3 1.0 copy-start.28
  121.3 2.0 copy-start.3
  122.3 80.6 %copy-start.29 = (f32[256]{0:T(256)S(1)}, f32[256]{0:T(256)}, u32[]{:S(2)}) copy-start(f32[256]{0:T(256)} %param.29) | copy-start | bytes 3076
  122.3 80.6 %copy-start.30 = (f32[256]{0:T(256)S(1)}, f32[256]{0:T(256)}, u32[]{:S(2)}) copy-start(f32[256]{0:T(256)} %param.25) | copy-start | bytes 3076
  125.1 79.8 %copy-start.14 = (f32[640,256]{1,0:T(8,128)S(1)}, f32[640,256]{1,0:T(8,128)}, u32[]{:S(2)}) copy-start(f32[640,256]{1,0:T(8,128)} %reduce-scatter.10.cloned.1.call-done) | copy-start | bytes 1966084
  152.9 52.0 %copy-start.15 = (f32[640,256]{1,0:T(8,128)S(1)}, f32[640,256]{1,0:T(8,128)}, u32[]{:S(2)}) copy-start(f32[640,256]{1,0:T(8,128)} %reduce-scatter.12.cloned.1.call-done) | copy-start | bytes 1966084
  192.6 328.6 %copy-start.31 = (f32[256]{0:T(256)}, f32[256]{0:T(256)S(1)}, u32[]{:S(2)}) copy-start(f32[256]{0:T(256)S(1)} %get-tuple-element.93) | copy-start | bytes 3076
Sparse Core Ops, SparseCore 0:
  9.6 21.0 all-gather.2
  32.2 18.3 all-gather.4
  81.7 34.3 reduce-scatter.9
  118.5 34.3 reduce-scatter.11
  155.3 34.3 reduce-scatter.7
  193.5 64.6 reduce-scatter.15
  262.4 73.9 reduce-scatter.13
  340.6 87.3 reduce-scatter.17
  432.3 88.2 reduce-scatter.19
where the time goes:
time: 529 us; the launch traced here: 528 us
  waiting for transfers between devices  369 us (70%)
  blocking collectives  47.8 us (9%)
  matrix products  47 us (9%)
  local copies, waits for them, and re-layouts  28.8 us (5%)
  other arithmetic  19.8 us (4%)
  between operations  14.9 us (3%)
    reduce_scatter x1, waiting for transfers between devices, body(): lax.psum_scatter(grad_contract, 'dp', scatter_dimension=1, tiled=True)  92.5 us
    reduce_scatter x1, waiting for transfers between devices, body(): lax.psum_scatter(grad_expand, 'dp', scatter_dimension=0, tiled=True)  91.6 us
    reduce_scatter x1, waiting for transfers between devices, body(): lax.psum_scatter(grad_heads, 'dp', scatter_dimension=0, tiled=True)  78.2 us
    reduce_scatter x1, waiting for transfers between devices, body(): lax.psum_scatter(grad_merge, 'dp', scatter_dimension=1, tiled=True)  50.9 us
    psum x1, blocking collectives, body(): lax.psum((gain_one, shift_one, gain_two, shift_two, grad_out_bias, grad_h...  37.6 us
    reduce_scatter x1, waiting for transfers between devices, body(): lax.psum_scatter(ffn_back, 'tensor', scatter_dimension=1, tiled=True)  27.8 us
    all_gather x1, waiting for transfers between devices, body(): lax.all_gather(hidden_states, 'tensor', axis=2, tiled=True)  16.7 us
    unnamed x76, local copies, waits for them, and re-layouts  11.6 us
  transfers between devices with their start and end apart: 9, of which 7 were waited for; matrix products, arithmetic and copies ran while one was open for 11% of the time, Pallas kernels for 0%

commit v1 on v0

--- a/solution.py
+++ b/solution.py
@@ -97,7 +97,7 @@
     cosine_table, sine_table = rotary_tables(length)
     residual = full_states.astype(jnp.float32).reshape(rows, width)
     normed_one, inverse_one, attn_norm = norm_forward(residual, gain_attention, shift_attention)
-    normed_two, inverse_two, ffn_norm = norm_forward(residual, gain_feedforward, shift_feedforward)
+    ffn_norm = normed_one * gain_feedforward + shift_feedforward
     attn_input = attn_norm.astype(jnp.bfloat16)
     ffn_input = ffn_norm.astype(jnp.bfloat16)
     flat_heads = heads_weight.reshape(width, 3 * local_width)
@@ -125,11 +125,11 @@
     active = gelu_value(pre_active).astype(jnp.bfloat16)
     ffn_part = jnp.dot(active, contract_weight, preferred_element_type=jnp.float32)
     summed = lax.psum_scatter(
-        (attn_part + ffn_part).reshape(slots, length, width),
+        (attn_part + ffn_part).astype(jnp.bfloat16).reshape(slots, length, width),
         "tensor",
         scatter_dimension=2,
         tiled=True,
-    )
+    ).astype(jnp.float32)
     block_output = (hidden_states.astype(jnp.float32) + summed + merge_bias + contract_bias).astype(
         jnp.bfloat16
     )
@@ -182,51 +182,54 @@
         width, 3, local_width
     )
     attn_back = jnp.dot(heads_grad16, flat_heads.T, preferred_element_type=jnp.float32)
-    sent_heads, sent_merge, sent_expand, sent_contract = (
-        lax.psum_scatter(grad_heads, "dp", scatter_dimension=0, tiled=True),
-        lax.psum_scatter(grad_merge, "dp", scatter_dimension=1, tiled=True),
-        lax.psum_scatter(grad_expand, "dp", scatter_dimension=0, tiled=True),
-        lax.psum_scatter(grad_contract, "dp", scatter_dimension=1, tiled=True),
-    )
-    share_one, share_two = (
-        lax.psum_scatter(attn_back, "tensor", scatter_dimension=1, tiled=True),
-        lax.psum_scatter(ffn_back, "tensor", scatter_dimension=1, tiled=True),
-    )
-    normed_one_own = own_columns(normed_one, start, local_width)
-    normed_two_own = own_columns(normed_two, start, local_width)
-    scaled_one = share_one * own_columns(gain_attention, start, local_width)
-    scaled_two = share_two * own_columns(gain_feedforward, start, local_width)
+    sent_contract, sent_expand, sent_merge, sent_heads = (
+        lax.psum_scatter(
+            grad_contract.astype(jnp.bfloat16), "dp", scatter_dimension=1, tiled=True
+        ).astype(jnp.float32),
+        lax.psum_scatter(
+            grad_expand.astype(jnp.bfloat16), "dp", scatter_dimension=0, tiled=True
+        ).astype(jnp.float32),
+        lax.psum_scatter(
+            grad_merge.astype(jnp.bfloat16), "dp", scatter_dimension=1, tiled=True
+        ).astype(jnp.float32),
+        lax.psum_scatter(
+            grad_heads.astype(jnp.bfloat16), "dp", scatter_dimension=0, tiled=True
+        ).astype(jnp.float32),
+    )
+    scaled = attn_back * gain_attention + ffn_back * gain_feedforward
     stats = lax.psum(
-        (
-            jnp.sum(scaled_one, axis=-1),
-            jnp.sum(scaled_one * normed_one_own, axis=-1),
-            jnp.sum(scaled_two, axis=-1),
-            jnp.sum(scaled_two * normed_two_own, axis=-1),
+        jnp.stack([jnp.sum(scaled, axis=-1), jnp.sum(scaled * normed_one, axis=-1)]), "tensor"
+    )
+    scaled_own = lax.psum_scatter(
+        scaled.astype(jnp.bfloat16), "tensor", scatter_dimension=1, tiled=True
+    ).astype(jnp.float32)
+    normed_own = own_columns(normed_one, start, local_width)
+    input_grad = own_masked + inverse_one * (
+        scaled_own - stats[0][:, None] / width - normed_own * (stats[1][:, None] / width)
+    )
+    norm_sums = lax.psum(
+        jnp.stack(
+            [
+                jnp.sum(attn_back * normed_one, axis=0),
+                jnp.sum(attn_back, axis=0),
+                jnp.sum(ffn_back * normed_one, axis=0),
+                jnp.sum(ffn_back, axis=0),
+            ]
         ),
-        "tensor",
-    )
-    input_one = inverse_one * (
-        scaled_one - stats[0][:, None] / width - normed_one_own * (stats[1][:, None] / width)
-    )
-    input_two = inverse_two * (
-        scaled_two - stats[2][:, None] / width - normed_two_own * (stats[3][:, None] / width)
-    )
-    input_grad = own_masked + input_one + input_two
-    gain_one = jnp.sum(share_one * normed_one_own, axis=0)
-    shift_one = jnp.sum(share_one, axis=0)
-    gain_two = jnp.sum(share_two * normed_two_own, axis=0)
-    shift_two = jnp.sum(share_two, axis=0)
-    vectors = lax.psum(
-        (
-            gain_one,
-            shift_one,
-            gain_two,
-            shift_two,
-            grad_out_bias,
-            grad_heads_bias,
-            grad_expand_bias,
-        ),
-        "dp",
+        ("dp", "tensor"),
+    )
+    norm_own = own_columns(norm_sums, start, local_width)
+    sums = lax.psum(
+        jnp.concatenate([grad_out_bias, grad_heads_bias.reshape(-1), grad_expand_bias]), "dp"
+    )
+    vectors = (
+        norm_own[0],
+        norm_own[1],
+        norm_own[2],
+        norm_own[3],
+        sums[:local_width],
+        sums[local_width : 4 * local_width].reshape(3, local_width),
+        sums[4 * local_width :],
     )
     input_grad = input_grad.astype(jnp.bfloat16).reshape(slots, length, local_width)
     return (

time: 529 us -> 419 us (0.79)
  waiting for transfers between devices: 369 us -> 219 us
  blocking collectives: 47.8 us -> 65.3 us
  local copies, waits for them, and re-layouts: 28.8 us -> 42.6 us
  other arithmetic: 19.8 us -> 25.6 us
    reduce_scatter x7 -> x4, waiting for transfers between devices: 341 us -> 125 us  [the longest x1 68.9 us: body(): lax.psum_scatter(grad_expand.astype(jnp.bfloat16), 'dp', scatter_dimensio...]
    unnamed x9 -> x10, waiting for transfers between devices: 1.49 us -> 70.5 us
    psum x2 -> x3, blocking collectives: 47.8 us -> 65.3 us  [the longest x1 36.9 us: body(): lax.psum(jnp.stack([jnp.sum(attn_back * normed_one, axis=0), jnp.sum(attn...]
    unnamed x76 -> x106, local copies, waits for them, and re-layouts: 11.6 us -> 21.4 us
    convert_element_type x0 -> x5, other arithmetic: none -> 6.28 us  [the longest x4 5 us: body(): sent_contract, sent_expand, sent_merge, sent_heads = (lax.psum_scatter(gr...]
  transfers between devices with their start and end apart: 9 -> 8, of which waited for: 7 -> 5; matrix products, arithmetic and copies ran while one was open for 11% -> 19% of each run, Pallas kernels for 0% -> 0%
where the time goes in v1:
time: 419 us; the launch traced here: 417 us
  waiting for transfers between devices  219 us (52%)
  blocking collectives  65.3 us (16%)
  matrix products  48 us (11%)
  local copies, waits for them, and re-layouts  42.6 us (10%)
  other arithmetic  25.6 us (6%)
  between operations  15.5 us (4%)
    unnamed x10, waiting for transfers between devices  70.5 us
    reduce_scatter x1, waiting for transfers between devices, body(): lax.psum_scatter(grad_expand.astype(jnp.bfloat16), 'dp', scatter_dimensio...  68.9 us
    reduce_scatter x1, waiting for transfers between devices, body(): lax.psum_scatter(grad_heads.astype(jnp.bfloat16), 'dp', scatter_dimension...  56 us
    psum x1, blocking collectives, body(): lax.psum(jnp.stack([jnp.sum(attn_back * normed_one, axis=0), jnp.sum(attn...  36.9 us
    psum x1, blocking collectives, body(): lax.psum(jnp.concatenate([grad_out_bias, grad_heads_bias.reshape(-1), gra...  21.6 us
    unnamed x106, local copies, waits for them, and re-layouts  21.4 us
    all_gather x1, waiting for transfers between devices, body(): lax.all_gather(hidden_states, 'tensor', axis=2, tiled=True)  16.7 us
  transfers between devices with their start and end apart: 8, of which 5 were waited for; matrix products, arithmetic and copies ran while one was open for 19% of the time, Pallas kernels for 0%

profile of v1, /device:TPU:0, one launch (start us, length us, event | category | flops | bytes accessed | tf_op | source)
XLA Modules:
  0.0 417.2 jit_solution(17755206777256663750)
XLA Ops:
  10.7 2.6 copy.48
  14.0 16.7 %all-gather.3.cloned.1.call-done = bf16[2,320,1024]{2,1,0:T(8,128)(2,1)} async-done(((bf16[2,320,256]{2,1,0:T(8,128)(2,1)}), bf16[2,320,1024]{2,1,0:T(8,128)(2,1)}) %all-gather.3.cloned.1.call-update) | async-done | bytes 1310736 | tf_op jit(solution)/shard_map/all_gather | solution.py:93
  30.6 1.7 convert_reduce_fusion
  33.0 1.8 multiply_reduce_fusion.3
  35.5 1.3 add_convert_fusion.2
  36.9 2.2 convolution_add_fusion
  39.1 1.4 copy-done.10
  43.2 7.4 %all-gather.5.cloned.1.call-done = bf16[2,320,1024]{2,1,0:T(8,128)(2,1)} async-done(((bf16[2,320,256]{2,1,0:T(8,128)(2,1)}), bf16[2,320,1024]{2,1,0:T(8,128)(2,1)}) %all-gather.5.cloned.1.call-update) | async-done | bytes 1310736 | tf_op jit(solution)/shard_map/all_gather | solution.py:94
  50.5 1.9 multiply_convert_fusion.1
  53.5 1.3 convolution_convert_fusion.5
  54.8 2.2 reshape.258
  57.0 2.0 copy.53
  60.2 2.0 select_reduce_fusion
  63.0 2.3 copy-done.11
  65.4 1.1 multiply_reduce_fusion.4
  66.5 2.6 multiply_convert_fusion
  69.2 1.1 copy.51
  70.3 2.0 reshape.248
  72.3 2.8 convolution_convert_fusion.3
  75.1 2.0 copy.70
  77.4 1.3 add_convert_fusion.1
  79.8 3.0 multiply_convert_fusion.2
  82.9 1.7 fusion.32
  85.3 1.5 fusion.38
  86.8 1.6 add_convert_fusion
  88.6 2.3 convolution_multiply_fusion
  95.1 2.2 copy.58
  97.4 3.6 convert_element_type.143
  100.9 5.1 %fusion.37 = (f32[1024]{0:T(1024)S(1)}, bf16[640,1024]{1,0:T(8,128)(2,1)S(1)}) fusion(f32[640,1024]{1,0:T(8,128)} %get-tuple-element.52, f32[1024]{0:T(1024)S(1)} %copy-done.47, bf16[640,1024]{1,0:T(8,128)(2,1)} %bitcast.124, bf16[1024,1024]{1,0:T(8,128)(2,1)} %param.28), kind=kOutput, calls=%fused_computation.93 | convolution fusion | flops 1350040576 | bytes 7348224 | tf_op jit(solution)/shard_map/dot_general | solution.py:145
  106.2 1.6 fusion.13
  108.3 5.0 %fusion.35 = (f32[640]{0:T(1024)}, f32[640]{0:T(1024)}, f32[1024]{0:T(1024)}, f32[1024]{0:T(1024)}, f32[1024]{0:T(1024)}, /*index=5*/f32[1024]{0:T(1024)}, bf16[640,1024]{1,0:T(8,128)(2,1)}, f32[640,1024]{1,0:T(8,128)}) fusion(f32[640]{0:T(1024)S(1)} %copy-done.36, f32[640]{0:T(1024)S(1)} %copy-done.37, bf16[2,320,1024]{2,1,0:T(8,128)(2,1)S(1)} %copy-done.3, ...), kind=kOutput, calls=%fused_computation.91 | convolution fusion | flops 1017113344 | bytes 10455040 | tf_op jit(solution)/shard_map/dot_general | solution.py:184
  113.4 4.3 %convolution_convert_fusion.2 = bf16[1024,3,256]{2,0,1:T(8,128)(2,1)} fusion(bf16[640,1024,1]{1,0,2:T(8,128)(2,1)} %bitcast.130, bf16[3,256,640]{2,1,0:T(8,128)(2,1)} %bitcast.131), kind=kOutput, calls=%fused_computation.28 | convolution fusion | flops 1007419392 | bytes 3866624 | tf_op jit(solution)/shard_map/dot_general | solution.py:181
  118.0 4.4 %convolution_convert_fusion = bf16[1024,1024]{1,0:T(8,128)(2,1)} fusion(bf16[640,1024]{1,0:T(8,128)(2,1)} %copy-done.48, bf16[640,1024]{1,0:T(8,128)(2,1)S(1)} %bitcast.125), kind=kOutput, calls=%fused_computation.26 | convolution fusion | flops 1343225856 | bytes 4718592 | tf_op jit(solution)/shard_map/dot_general | solution.py:144
  122.4 4.0 copy.72
  126.6 4.5 %convolution_convert_fusion.1 = bf16[1024,1024]{1,0:T(8,128)(2,1)} fusion(bf16[640,1024]{1,0:T(8,128)(2,1)S(1)} %copy-done.23, bf16[640,1024]{1,0:T(8,128)(2,1)} %copy-done.49), kind=kOutput, calls=%fused_computation.27 | convolution fusion | flops 1343225856 | bytes 4718592 | tf_op jit(solution)/shard_map/dot_general | solution.py:150
  131.1 1.8 fusion.31
  132.9 1.6 fusion.7
  135.3 21.6 %psum.23 = f32[2048]{0:T(1024)S(1)} all-reduce(f32[2048]{0:T(1024)S(1)} %pad_maximum_fusion.4), channel_id=1, replica_groups=mesh['dp'=8,'tensor'=4] {'dp'}, use_global_device_ids=true, to_apply=%region_19.20 | all-reduce | flops 2048 | bytes 16384 | tf_op jit(solution)/shard_map/psum | solution.py:222
  159.4 6.8 %psum.21 = f32[2,640]{1,0:T(2,128)S(1)} all-reduce(f32[2,640]{1,0:T(2,128)S(1)} %pad_maximum_fusion.5), channel_id=1, replica_groups=mesh['dp'=8,'tensor'=4] {'tensor'}, use_global_device_ids=true, to_apply=%region_9.10 | all-reduce | flops 1280 | bytes 10240 | tf_op jit(solution)/shard_map/psum | solution.py:200
  167.0 36.9 %psum.22 = f32[4,1024]{1,0:T(4,128)S(1)} all-reduce(f32[4,1024]{1,0:T(4,128)S(1)} %pad_maximum_fusion.3), channel_id=1, replica_groups=mesh['dp'=8,'tensor'=4] {'dp','tensor'}, use_global_device_ids=true, to_apply=%region_14.15 | all-reduce | flops 4096 | bytes 32768 | tf_op jit(solution)/shard_map/psum | solution.py:210
  206.3 1.9 add_convert_fusion.3
  208.2 2.3 fusion.11
  210.5 56.0 %reduce-scatter.15.cloned.1.call-done = bf16[128,3,256]{2,0,1:T(8,128)(2,1)} async-done(((bf16[1024,3,256]{2,0,1:T(8,128)(2,1)}), bf16[128,3,256]{2,0,1:T(8,128)(2,1)}) %reduce-scatter.15.cloned.1.call-update) | async-done | bytes 196624 | tf_op jit(solution)/shard_map/reduce_scatter | solution.py:195
  266.5 1.7 convert_element_type.150
  268.2 69.0 %reduce-scatter.21.cloned.1.call-done = bf16[128,1024]{1,0:T(8,128)(2,1)} async-done(((bf16[1024,1024]{1,0:T(8,128)(2,1)}), bf16[128,1024]{1,0:T(8,128)(2,1)}) %reduce-scatter.21.cloned.1.call-update) | async-done | bytes 262160
  337.2 1.1 copy.73
  339.1 68.9 %reduce-scatter.17.cloned.1.call-done = bf16[128,1024]{1,0:T(8,128)(2,1)} async-done(((bf16[1024,1024]{1,0:T(8,128)(2,1)}), bf16[128,1024]{1,0:T(8,128)(2,1)}) %reduce-scatter.17.cloned.1.call-update) | async-done | bytes 262160 | tf_op jit(solution)/shard_map/reduce_scatter | solution.py:189
  408.0 1.8 convert_element_type.154
  (155 shorter events, 25.7 us)
Async XLA Ops:
  7.2 72.6 %copy-start = (bf16[1024,1024]{1,0:T(8,128)(2,1)S(1)}, bf16[1024,1024]{1,0:T(8,128)(2,1)}, u32[]{:S(2)}) copy-start(bf16[1024,1024]{1,0:T(8,128)(2,1)} %param.26) | copy-start | bytes 6291460
  7.2 6.0 %copy-start.41 = (f32[3,256]{1,0:T(4,128)S(1)}, f32[3,256]{1,0:T(4,128)}, u32[]{:S(2)}) copy-start(f32[3,256]{1,0:T(4,128)} %param.23) | copy-start | bytes 9220
  7.2 23.4 %all-gather.3.cloned.1.call-start = ((), (), s32[]{:S(2)}) async-start(), calls=%async_computation.6 | async-start | bytes 1638400 | tf_op jit(solution)/shard_map/all_gather | solution.py:93
  7.9 42.6 %all-gather.5.cloned.1.call-start = ((), (), s32[]{:S(2)}) async-start(), calls=%async_computation.8 | async-start | bytes 1638400 | tf_op jit(solution)/shard_map/all_gather | solution.py:94
  8.7 195.9 %reduce-scatter.19.cloned.1.call-start = ((), (), s32[]{:S(2)}) async-start(), calls=%async_computation.12 | async-start | bytes 589824
  10.6 24.8 %copy-start.38 = (f32[1024]{0:T(1024)S(1)}, f32[1024]{0:T(1024)}, u32[]{:S(2)}) copy-start(f32[1024]{0:T(1024)} %param.19) | copy-start | bytes 12292
  30.6 4.8 %copy-start.3 = (bf16[2,320,1024]{2,1,0:T(8,128)(2,1)S(1)}, bf16[2,320,1024]{2,1,0:T(8,128)(2,1)}, u32[]{:S(2)}) copy-start(bf16[2,320,1024]{2,1,0:T(8,128)(2,1)} %all-gather.3.cloned.1.call-done) | copy-start | bytes 3932164
  36.8 2.2 copy-start.24
  40.5 10.0 %copy-start.43 = (f32[2]{0:T(128)S(1)}, f32[2]{0:T(128)}, u32[]{:S(2)}) copy-start(f32[2]{0:T(128)} %compare_convert_fusion) | copy-start | bytes 28
  40.7 1.7 copy-start.19
  50.5 3.0 copy-start.26
  52.4 6.6 %copy-start.35 = (f32[320,8]{0,1:T(8,128)S(1)}, f32[320,8]{0,1:T(8,128)}, u32[]{:S(2)}) copy-start(f32[320,8]{0,1:T(8,128)} %get-tuple-element.49) | copy-start | bytes 30724
  60.1 2.1 copy-start.28
  60.1 2.1 copy-start.30
  60.1 2.1 copy-start.32
  60.1 2.1 copy-start.33
  62.2 4.3 %copy-start.1 = (f32[2,4,320,320]{2,3,1,0:T(8,128)}, f32[2,4,320,320]{2,3,1,0:T(8,128)S(1)}, u32[]{:S(2)}) copy-start(f32[2,4,320,320]{2,3,1,0:T(8,128)S(1)} %get-tuple-element.54) | copy-start | bytes 9830404
  62.2 3.1 copy-start.11
  62.3 3.1 copy-start.12
  77.2 129.1 %reduce-scatter.11.cloned.1.call-start = ((), (), s32[]{:S(2)}) async-start(), calls=%async_computation.7 | async-start | bytes 1638400 | tf_op jit(solution)/shard_map/reduce_scatter | solution.py:127
  77.4 2.4 copy-start.46
  79.8 3.1 copy-start.4
  79.8 3.1 copy-start.18
  79.8 3.1 copy-start.29
  79.8 3.1 copy-start.31
  82.9 3.9 copy-start.48
  82.9 2.4 copy-start.45
  88.5 119.7 %reduce-scatter.13.cloned.1.call-start = ((), (), s32[]{:S(2)}) async-start(), calls=%async_computation.9 | async-start | bytes 1638400 | tf_op jit(solution)/shard_map/reduce_scatter | solution.py:203
  88.5 2.4 copy-start.15
  88.5 2.4 copy-start.34
  90.8 2.3 copy-start.2
  90.8 2.4 copy-start.13
  95.1 5.8 %copy-start.47 = (f32[1024]{0:T(1024)S(1)}, f32[1024]{0:T(1024)}, u32[]{:S(2)}) copy-start(f32[1024]{0:T(1024)} %param.27) | copy-start | bytes 12292
  106.1 1.6 copy-start.49
  106.1 1.9 copy-start.21
  106.1 2.2 copy-start.25
  106.1 2.2 copy-start.36
  106.1 2.1 copy-start.37
  106.1 2.1 copy-start.39
  106.2 2.1 copy-start.40
  113.3 153.2 %reduce-scatter.15.cloned.1.call-start = ((), (), s32[]{:S(2)}) async-start(), calls=%async_computation.10 | async-start | bytes 1769472 | tf_op jit(solution)/shard_map/reduce_scatter | solution.py:195
  113.3 4.6 %copy-start.9 = (bf16[2,320,1024]{2,1,0:T(8,128)(2,1)S(1)}, bf16[2,320,1024]{2,1,0:T(8,128)(2,1)}, u32[]{:S(2)}) copy-start(bf16[2,320,1024]{2,1,0:T(8,128)(2,1)} %copy-done.8) | copy-start | bytes 3932164
  117.7 219.5 %reduce-scatter.21.cloned.1.call-start = ((), (), s32[]{:S(2)}) async-start(), calls=%async_computation.13 | async-start | bytes 2359296
  122.4 4.1 copy-start.23
  126.5 4.6 %copy-start.44 = (f32[2]{0:T(128)S(1)}, f32[2]{0:T(128)}, u32[]{:S(2)}) copy-start(f32[2]{0:T(128)} %compare_convert_fusion) | copy-start | bytes 28
  126.5 281.5 %reduce-scatter.17.cloned.1.call-start = ((), (), s32[]{:S(2)}) async-start(), calls=%async_computation.11 | async-start | bytes 2359296 | tf_op jit(solution)/shard_map/reduce_scatter | solution.py:189
  131.1 1.9 copy-start.6
  157.5 252.3 %copy-start.42 = (f32[256]{0:T(256)}, f32[256]{0:T(256)S(1)}, u32[]{:S(2)}) copy-start(f32[256]{0:T(256)S(1)} %slice.127) | copy-start | bytes 3076
  (11 other events, 13.2 us)
Sparse Core Ops, SparseCore 0:
  9.6 21.0 all-gather.2
  32.2 18.3 all-gather.4
  77.3 62.5 reduce-scatter.18
  142.3 25.6 reduce-scatter.10
  170.4 26.3 reduce-scatter.12
  200.1 66.3 reduce-scatter.14
  270.0 67.0 reduce-scatter.20
  340.7 67.2 reduce-scatter.16
